TPU v7x, 256 devices: a whole 4x4x8 slice. The times are simulated.
256 devices in a mesh: row: 16 (over z, core), col: 16 (over x, y).
Axes of the slice: x: 4, y: 4, z: 8, core: 2. Of those that a mesh axis runs over, the one named last changes fastest.
Arguments:
- tokens: bfloat16 [4096, 8192], P('row', 'col'), may hold values from -6 to 6
- out_grad: bfloat16 [4096, 8192], P('row', 'col'), may hold values from -1.5 to 1.5
- gate_weight: bfloat16 [112, 1024, 128], P('col', 'row'), may hold values from -0.1875 to 0.1875
- up_weight: bfloat16 [112, 1024, 128], P('col', 'row'), may hold values from -0.1875 to 0.1875
- down_weight: bfloat16 [112, 1024, 128], P('col', 'row'), may hold values from -0.125 to 0.125
- gate_rows: int32 [112, 8], P('col'), may hold values from 0 to 63, all different within a row
- up_rows: int32 [112, 8], P('col'), may hold values from 0 to 63, all different within a row
- down_columns: int32 [112, 8], P('col'), may hold values from 0 to 63, all different within a row
Outputs:
- output: bfloat16 [4096, 8192], P('row', 'col')
- input_grad: bfloat16 [4096, 8192], P('row', 'col')
- gate_weight_grad: bfloat16 [112, 1024, 128], P('col', 'row')
- up_weight_grad: bfloat16 [112, 1024, 128], P('col', 'row')
- down_weight_grad: bfloat16 [112, 1024, 128], P('col', 'row')
Inputs may be any that keep to these rules, and one draw needn't show every extreme that they name: `gate_rows`: each row names 8 different block-rows; every block-row is named in some row. `up_rows`: each row names 8 different block-rows; every block-row is named in some row. `down_columns`: each row names 8 different output block-columns; every block-column is named in some row.
All inputs are finite; a program needn't handle non-finite values.
Results may differ from a plain program's by a relative error of at most 0.018.
Values may be sent and summed in bfloat16 or wider, within the bound.
A program may use at most 128 MiB of HBM per device.

v0:
```python
import jax
import jax.numpy as jnp
from jax import lax
from jax.sharding import PartitionSpec as P

D = 8192
BS = 128
KG = 8
KH = 8
DB = 64


def spread(contrib, block_lists):
    rows_here = contrib.shape[0]
    zero_block = jnp.zeros((rows_here, DB, BS), jnp.float32)
    placed = zero_block.at[:, block_lists.reshape(-1)].add(contrib.reshape(rows_here, -1, BS))
    return placed.reshape(rows_here, D)


def shards(tokens, out_grad, gate_weight, up_weight, down_weight, gate_rows, up_rows, down_columns):
    panels = lax.all_gather(jnp.stack([tokens, out_grad]), "col", axis=2, tiled=True)
    panel_in, panel_grad = (panels[0], panels[1])
    rows_here = panel_in.shape[0]
    owned_slots = gate_weight.shape[0]
    tiles = lax.all_gather(
        jnp.concatenate([gate_weight, up_weight, down_weight], axis=0), "row", axis=1, tiled=True
    )
    gate_tiles = tiles[:owned_slots]
    up_tiles = tiles[owned_slots : 2 * owned_slots]
    down_tiles = tiles[2 * owned_slots :]
    gate_four = gate_tiles.reshape(owned_slots, KG, BS, BS)
    up_four = up_tiles.reshape(owned_slots, KG, BS, BS)
    blocks_in = panel_in.reshape(rows_here, DB, BS)
    picked_gate = jnp.take(blocks_in, gate_rows.reshape(-1), axis=1).reshape(
        rows_here, owned_slots, KG, BS
    )
    picked_up = jnp.take(blocks_in, up_rows.reshape(-1), axis=1).reshape(
        rows_here, owned_slots, KG, BS
    )
    gate_value = jnp.einsum(
        "tfkr,fkri->tfi", picked_gate, gate_four, preferred_element_type=jnp.float32
    )
    up_value = jnp.einsum("tfkr,fkri->tfi", picked_up, up_four, preferred_element_type=jnp.float32)
    sigmoid_gate = jax.nn.sigmoid(gate_value)
    silu_gate = gate_value * sigmoid_gate
    hidden = (silu_gate * up_value).astype(jnp.bfloat16)
    down_four = down_tiles.reshape(owned_slots, KH, BS, BS)
    out_part = jnp.einsum("tfi,fkji->tfkj", hidden, down_four, preferred_element_type=jnp.float32)
    partial_out = spread(out_part, down_columns)
    blocks_grad = panel_grad.reshape(rows_here, DB, BS)
    picked_grad = jnp.take(blocks_grad, down_columns.reshape(-1), axis=1).reshape(
        rows_here, owned_slots, KH, BS
    )
    hidden_grad = jnp.einsum(
        "tfkj,fkji->tfi", picked_grad, down_four, preferred_element_type=jnp.float32
    )
    gate_grad = (
        hidden_grad * up_value * sigmoid_gate * (1.0 + gate_value * (1.0 - sigmoid_gate))
    ).astype(jnp.bfloat16)
    up_grad = (hidden_grad * silu_gate).astype(jnp.bfloat16)
    from_gate = jnp.einsum(
        "tfi,fkri->tfkr", gate_grad, gate_four, preferred_element_type=jnp.float32
    )
    from_up = jnp.einsum("tfi,fkri->tfkr", up_grad, up_four, preferred_element_type=jnp.float32)
    partial_in = spread(from_gate, gate_rows) + spread(from_up, up_rows)
    gate_partial = jnp.einsum(
        "tfkr,tfi->fkri", picked_gate, gate_grad, preferred_element_type=jnp.float32
    ).reshape(owned_slots, KG * BS, BS)
    up_partial = jnp.einsum(
        "tfkr,tfi->fkri", picked_up, up_grad, preferred_element_type=jnp.float32
    ).reshape(owned_slots, KG * BS, BS)
    down_partial = jnp.einsum(
        "tfkj,tfi->fkji", picked_grad, hidden, preferred_element_type=jnp.float32
    ).reshape(owned_slots, KH * BS, BS)
    tile_sums = lax.psum_scatter(
        jnp.concatenate([gate_partial, up_partial, down_partial], axis=0).astype(jnp.bfloat16),
        "row",
        scatter_dimension=1,
        tiled=True,
    )
    panel_sums = lax.psum_scatter(
        jnp.stack([partial_out, partial_in]).astype(jnp.bfloat16),
        "col",
        scatter_dimension=2,
        tiled=True,
    )
    return (
        panel_sums[0],
        panel_sums[1],
        tile_sums[:owned_slots],
        tile_sums[owned_slots : 2 * owned_slots],
        tile_sums[2 * owned_slots :],
    )


def solution(mesh):
    in_specs = (
        P("row", "col"),
        P("row", "col"),
        P("col", "row", None),
        P("col", "row", None),
        P("col", "row", None),
        P("col", None),
        P("col", None),
        P("col", None),
    )
    out_specs = (
        P("row", "col"),
        P("row", "col"),
        P("col", "row", None),
        P("col", "row", None),
        P("col", "row", None),
    )
    return jax.shard_map(shards, mesh=mesh, in_specs=in_specs, out_specs=out_specs, check_vma=False)
```

profile of v0, /device:TPU:2, one launch (start us, length us, event | category | flops | bytes accessed | tf_op | source)
XLA Modules:
  0.0 436.0 jit_solution(9459463797062491396)
XLA Ops:
  7.2 0.0 all-gather.3.cloned.1.call-start
  7.2 1.8 pad_maximum_fusion.3
  9.0 0.0 all-gather.3.cloned.1.call-update
  9.0 0.0 all-gather.5.cloned.1.call-start
  9.1 1.1 copy.50
  10.2 1.1 copy.51
  11.3 0.8 pad_maximum_fusion.2
  12.1 0.0 reduce-scatter.5.cloned.1.call-start
  12.2 0.8 reshape.183
  13.0 0.1 reshape.187
  13.0 0.1 reshape.180
  13.2 43.8 %all-gather.3.cloned.1.call-done = bf16[21,1024,128]{2,1,0:T(8,128)(2,1)} async-done(((bf16[21,64,128]{2,1,0:T(8,128)(2,1)}), bf16[21,1024,128]{2,1,0:T(8,128)(2,1)}) %all-gather.3.cloned.1.call-update) | async-done | bytes 5505040 | tf_op jit(solution)/shard_map/all_gather | solution.py:25
  57.1 4.9 %fusion.10 = (bf16[7,1024,128]{2,1,0:T(8,128)(2,1)}, bf16[7,1024,128]{2,1,0:T(8,128)(2,1)}, bf16[7,1024,128]{2,1,0:T(8,128)(2,1)S(1)}) fusion(bf16[21,1024,128]{2,1,0:T(8,128)(2,1)} %all-gather.3.cloned.1.call-done), kind=kLoop, calls=%fused_computation.48 | loop fusion | bytes 11010048 | tf_op jit(solution)/shard_map/slice | solution.py:29
  61.9 71.8 %all-gather.5.cloned.1.call-done = bf16[2,256,8192]{1,2,0:T(8,128)(2,1)} async-done(((bf16[2,256,512]{1,2,0:T(8,128)(2,1)}), bf16[2,256,8192]{1,2,0:T(8,128)(2,1)}) %all-gather.5.cloned.1.call-update) | async-done | bytes 8388624 | tf_op jit(solution)/shard_map/all_gather | solution.py:21
  133.7 5.7 %fusion.9 = (bf16[1,256,8192]{1,2,0:T(8,128)(2,1)}, bf16[1,256,8192]{1,2,0:T(8,128)(2,1)}) fusion(bf16[2,256,8192]{1,2,0:T(8,128)(2,1)} %all-gather.5.cloned.1.call-done), kind=kLoop, calls=%fused_computation.47 | loop fusion | bytes 16777216 | tf_op jit(solution)/shard_map/slice | solution.py:22
  139.4 6.4 %copy.52 = bf16[256,64,128]{2,0,1:T(8,128)(2,1)} copy(bf16[256,64,128]{0,2,1:T(8,128)(2,1)} %bitcast.106) | data formatting | bytes 8388608 | tf_op jit(solution)/shard_map/reshape;squeeze | solution.py:33
  145.9 6.4 %copy.59 = bf16[256,64,128]{2,0,1:T(8,128)(2,1)} copy(bf16[256,64,128]{0,2,1:T(8,128)(2,1)} %bitcast.105) | data formatting | bytes 8388608 | tf_op jit(solution)/shard_map/reshape;squeeze | solution.py:50
  152.2 5.1 %gather_fusion.1 = bf16[56,256,128]{2,1,0:T(8,128)(2,1)} fusion(bf16[256,64,128]{2,0,1:T(8,128)(2,1)} %copy.52, s32[1024]{0:T(1024)S(1)} %pad_clamp_fusion.1), kind=kCustom, calls=%fused_computation.1.clone | custom fusion | bytes 7340256 | tf_op jit(solution)/shard_map/jit(_take)/gather | solution.py:37
  157.3 5.1 %gather_fusion = bf16[56,256,128]{2,1,0:T(8,128)(2,1)} fusion(bf16[256,64,128]{2,0,1:T(8,128)(2,1)} %copy.52, s32[1024]{0:T(1024)S(1)} %pad_clamp_fusion.2), kind=kCustom, calls=%fused_computation.clone | custom fusion | bytes 7340256 | tf_op jit(solution)/shard_map/jit(_take)/gather | solution.py:34
  162.4 2.6 broadcast_select_fusion.1
  165.0 1.8 copy-done
  166.8 2.3 convolution_bitcast_fusion.1
  169.0 5.1 %gather_fusion.2 = bf16[56,256,128]{2,1,0:T(8,128)(2,1)} fusion(bf16[256,64,128]{2,0,1:T(8,128)(2,1)} %copy.59, s32[1024]{0:T(1024)S(1)} %pad_clamp_fusion), kind=kCustom, calls=%fused_computation.2.clone | custom fusion | bytes 7340256 | tf_op jit(solution)/shard_map/jit(_take)/gather | solution.py:51
  174.1 2.4 broadcast_select_fusion
  176.6 1.4 convolution_bitcast_fusion
  177.9 0.7 copy-done.3
  178.6 0.4 broadcast_select_fusion.2
  179.0 1.1 copy-done.4
  180.1 0.2 copy-done.5
  180.3 1.6 fusion.1
  181.9 1.4 convolution_convert_fusion.2
  183.3 0.7 copy-done.1
  184.0 1.4 convolution_convert_fusion.1
  185.3 1.4 convolution_convert_fusion
  186.7 2.9 pad_maximum_fusion.1
  189.6 0.0 reduce-scatter.5.cloned.1.call-update
  189.6 0.2 reduce-scatter.3.cloned.1.call-start
  189.9 0.4 copy-done.6
  190.3 0.1 reshape.190
  190.4 0.1 reshape.186
  190.5 0.1 reshape.177
  190.6 5.6 %fusion.13 = f32[7,8,128,256]{3,2,1,0:T(8,128)} fusion(bf16[7,8,128,128]{3,2,1,0:T(8,128)(2,1)} %bitcast.110, bf16[256,7,128,1]{0,2,3,1:T(8,128)(2,1)S(1)} %get-tuple-element.23), kind=kOutput, calls=%fused_computation.51 | convolution fusion | flops 469762048 | bytes 9633792 | tf_op jit(solution)/shard_map/tfi,fkri->tfkr/dot_general | solution.py:64
  196.2 8.4 %copy.64 = f32[256,56,128]{2,0,1:T(8,128)} copy(f32[256,56,128]{0,2,1:T(8,128)} %bitcast.98) | data formatting | bytes 14680064 | tf_op jit(solution)/shard_map/reshape | solution.py:16
  204.6 5.6 %fusion.4 = f32[7,8,128,256]{3,2,1,0:T(8,128)} fusion(bf16[7,8,128,128]{3,2,1,0:T(8,128)(2,1)} %bitcast.114, bf16[256,7,128]{0,2,1:T(8,128)(2,1)S(1)} %get-tuple-element.22), kind=kOutput, calls=%fused_computation.27 | convolution fusion | flops 469762048 | bytes 9633792 | tf_op jit(solution)/shard_map/tfi,fkri->tfkr/dot_general | solution.py:61
  210.2 8.4 %copy.62 = f32[256,56,128]{2,0,1:T(8,128)} copy(f32[256,56,128]{0,2,1:T(8,128)} %bitcast.99) | data formatting | bytes 14680064 | tf_op jit(solution)/shard_map/reshape | solution.py:16
  218.6 4.3 broadcast.57.clone.1
  222.8 19.0 %scatter_fusion.2 = f32[256,64,128]{2,0,1:T(8,128)} fusion(f32[256,64,128]{2,0,1:T(8,128)} %broadcast.57.clone.1, s32[56]{0:T(128)S(1)} %fusion.8, f32[56,256,128]{2,1,0:T(8,128)} %bitcast.101), kind=kCustom, calls=%fused_computation.5 | custom fusion | flops 1835008 | bytes 22020320 | tf_op jit(solution)/shard_map/scatter-add | solution.py:16
  241.8 4.2 broadcast.57.clone
  246.1 19.1 %scatter_fusion.1 = f32[256,64,128]{2,0,1:T(8,128)} fusion(f32[256,64,128]{2,0,1:T(8,128)} %broadcast.57.clone, s32[56]{0:T(128)S(1)} %fusion.7, f32[56,256,128]{2,1,0:T(8,128)} %bitcast.102), kind=kCustom, calls=%fused_computation.4 | custom fusion | flops 1835008 | bytes 22020320 | tf_op jit(solution)/shard_map/scatter-add | solution.py:16
  265.2 9.5 %add_convert_fusion = bf16[256,64,128]{2,0,1:T(8,128)(2,1)} fusion(f32[256,64,128]{2,0,1:T(8,128)} %scatter_fusion.1, f32[256,64,128]{2,0,1:T(8,128)} %scatter_fusion.2), kind=kLoop, calls=%fused_computation.7 | loop fusion | flops 4194304 | bytes 20971520 | tf_op jit(solution)/shard_map/convert.8
  274.7 6.4 %copy.65 = bf16[256,64,128]{0,2,1:T(8,128)(2,1)} copy(bf16[256,64,128]{2,0,1:T(8,128)(2,1)} %add_convert_fusion) | data formatting | bytes 8388608 | tf_op jit(solution)/shard_map/convert.8
  281.1 4.0 fusion.12
  285.2 8.3 %copy.57 = f32[256,56,128]{2,0,1:T(8,128)} copy(f32[256,56,128]{0,2,1:T(8,128)} %bitcast.100) | data formatting | bytes 14680064 | tf_op jit(solution)/shard_map/reshape | solution.py:16
  293.5 4.2 broadcast.57.clone.2
  297.7 18.8 %scatter_fusion = f32[256,64,128]{2,0,1:T(8,128)} fusion(f32[256,64,128]{2,0,1:T(8,128)} %broadcast.57.clone.2, s32[56]{0:T(128)S(1)} %fusion.6, f32[56,256,128]{2,1,0:T(8,128)} %bitcast.103), kind=kCustom, calls=%fused_computation.3 | custom fusion | flops 1835008 | bytes 22020320 | tf_op jit(solution)/shard_map/scatter-add | solution.py:16
  316.6 6.1 %convert.20 = bf16[256,64,128]{2,0,1:T(8,128)(2,1)} convert(f32[256,64,128]{2,0,1:T(8,128)} %scatter_fusion) | non-fusion elementwise | flops 2097152 | bytes 12582912 | tf_op jit(solution)/shard_map/convert.9
  322.7 6.4 %copy.58 = bf16[256,64,128]{0,2,1:T(8,128)(2,1)} copy(bf16[256,64,128]{2,0,1:T(8,128)(2,1)} %convert.20) | data formatting | bytes 8388608 | tf_op jit(solution)/shard_map/convert.9
  329.0 7.4 %pad_maximum_fusion = bf16[2,256,8192]{1,2,0:T(8,128)(2,1)} fusion(bf16[1,256,8192]{1,2,0:T(8,128)(2,1)} %bitcast.104, bf16[1,256,8192]{1,2,0:T(8,128)(2,1)} %bitcast.107), kind=kLoop, calls=%fused_computation.6 | loop fusion | flops 4194304 | bytes 16777216 | tf_op jit(solution)/shard_map/stack | solution.py:82
  336.5 0.0 reduce-scatter.5.cloned.1.call-done
  336.5 1.7 fusion.11
  338.3 88.4 %reduce-scatter.3.cloned.1.call-done = bf16[2,256,512]{1,2,0:T(8,128)(2,1)} async-done(((bf16[2,256,8192]{1,2,0:T(8,128)(2,1)}), bf16[2,256,512]{1,2,0:T(8,128)(2,1)}) %reduce-scatter.3.cloned.1.call-update) | async-done | bytes 524304 | tf_op jit(solution)/shard_map/reduce_scatter | solution.py:81
  426.7 1.1 slice_bitcast_fusion
  427.7 0.8 copy.72
  428.6 0.8 copy.73
  (26 shorter events, 0.1 us)
Async XLA Ops:
  7.2 5.8 %copy-start.8 = (s32[7,8]{1,0:T(8,128)S(1)}, s32[7,8]{1,0:T(8,128)}, u32[]{:S(2)}) copy-start(s32[7,8]{1,0:T(8,128)} %param.17) | copy-start | bytes 676
  7.2 5.9 %copy-start.7 = (s32[7,8]{1,0:T(8,128)S(1)}, s32[7,8]{1,0:T(8,128)}, u32[]{:S(2)}) copy-start(s32[7,8]{1,0:T(8,128)} %param.15) | copy-start | bytes 676
  7.2 49.9 %all-gather.3.cloned.1.call-start = ((), (), s32[]{:S(2)}) async-start(), calls=%async_computation.2 | async-start | bytes 5849088 | tf_op jit(solution)/shard_map/all_gather | solution.py:25
  9.0 124.7 %all-gather.5.cloned.1.call-start = ((), (), s32[]{:S(2)}) async-start(), calls=%async_computation.3 | async-start | bytes 8912896 | tf_op jit(solution)/shard_map/all_gather | solution.py:21
  12.1 324.4 %reduce-scatter.5.cloned.1.call-start = ((), (), s32[]{:S(2)}) async-start(), calls=%async_computation.5 | async-start | bytes 5849088 | tf_op jit(solution)/shard_map/reduce_scatter | solution.py:75
  162.4 4.4 %copy-start.2 = (bf16[7,1024,128]{2,1,0:T(8,128)(2,1)S(1)}, bf16[7,1024,128]{2,1,0:T(8,128)(2,1)}, u32[]{:S(2)}) copy-start(bf16[7,1024,128]{2,1,0:T(8,128)(2,1)} %get-tuple-element.18) | copy-start | bytes 5505028
  164.9 1.8 copy-start
  176.5 2.0 copy-start.3
  178.6 1.5 copy-start.4
  178.6 1.7 copy-start.5
  181.9 2.0 copy-start.1
  189.6 0.7 copy-start.6
  189.6 237.0 %reduce-scatter.3.cloned.1.call-start = ((), (), s32[]{:S(2)}) async-start(), calls=%async_computation.4 | async-start | bytes 8912896 | tf_op jit(solution)/shard_map/reduce_scatter | solution.py:81
Sparse Core Ops, SparseCore 0:
  9.9 47.1 all-gather.2
  59.6 74.1 all-gather.4
  189.8 64.9 reduce-scatter.4
  336.6 89.9 reduce-scatter.2
where the time goes:
time: 438 us; the launch traced here: 436 us
  waiting for transfers between devices  204 us (47%)
  local copies, waits for them, and re-layouts  102 us (23%)
  other arithmetic  91 us (21%)
  matrix products  24.6 us (6%)
  between operations  14 us (3%)
    reduce_scatter x1, waiting for transfers between devices, shards(): lax.psum_scatter(jnp.stack([partial_out, partial_in]).astype(jnp.bfloat16...  88.4 us
    all_gather x1, waiting for transfers between devices, shards(): lax.all_gather(jnp.stack([tokens, out_grad]), 'col', axis=2, tiled=True)  71.8 us
    scatter-add x3, other arithmetic, spread(): zero_block.at[:, block_lists.reshape(-1)]  56.9 us
    all_gather x1, waiting for transfers between devices, shards(): lax.all_gather(jnp.concatenate([gate_weight, up_weight, down_weight], axi...  43.8 us
    another operation x5, local copies, waits for them, and re-layouts  25.5 us
    reshape x3, local copies, waits for them, and re-layouts, spread(): contrib.reshape(rows_here, -1, BS)  25.1 us
    another operation x2, other arithmetic  15.6 us
  transfers between devices with their start and end apart: 4, of which 3 were waited for; matrix products, arithmetic and copies ran while one was open for 36% of the time, Pallas kernels for 0%

commit v1 on v0

--- a/solution.py
+++ b/solution.py
@@ -22,8 +22,17 @@
     panel_in, panel_grad = (panels[0], panels[1])
     rows_here = panel_in.shape[0]
     owned_slots = gate_weight.shape[0]
-    tiles = lax.all_gather(
-        jnp.concatenate([gate_weight, up_weight, down_weight], axis=0), "row", axis=1, tiled=True
+    tiles = jnp.concatenate(
+        lax.all_to_all(
+            jnp.stack(
+                [jnp.concatenate([gate_weight, up_weight, down_weight], axis=0)]
+                * lax.axis_size("row")
+            ),
+            "row",
+            0,
+            0,
+        ),
+        axis=1,
     )
     gate_tiles = tiles[:owned_slots]
     up_tiles = tiles[owned_slots : 2 * owned_slots]

time: 438 us -> 456 us (1.041)
  starting transfers between devices: 0.34 us -> 8.87 us
  waiting for transfers between devices: 204 us -> 210 us
  local copies, waits for them, and re-layouts: 102 us -> 107 us
    all_to_all x0 -> x1, waiting for transfers between devices: none -> 122 us  [shards(): lax.all_to_all(jnp.stack([jnp.concatenate([gate_weight, up_weight, down_w...]
    all_gather x1, waiting for transfers between devices: 71.8 us -> 0.01 us  [shards(): lax.all_gather(jnp.stack([tokens, out_grad]), 'col', axis=2, tiled=True)]
    all_gather x1 -> x0, waiting for transfers between devices: 43.8 us -> none  [shards(): lax.all_gather(jnp.concatenate([gate_weight, up_weight, down_weight], axi...]
    all_to_all x0 -> x1, starting transfers between devices: none -> 8.75 us  [shards(): lax.all_to_all(jnp.stack([jnp.concatenate([gate_weight, up_weight, down_w...]
    another operation x5 -> x6, local copies, waits for them, and re-layouts: 25.5 us -> 29.3 us
  transfers between devices with their start and end apart: 4 -> 4, of which waited for: 3 -> 2; matrix products, arithmetic and copies ran while one was open for 36% -> 35% of each run, Pallas kernels for 0% -> 0%
where the time goes in v1:
time: 456 us; the launch traced here: 454 us
  waiting for transfers between devices  210 us (46%)
  local copies, waits for them, and re-layouts  107 us (23%)
  other arithmetic  90.4 us (20%)
  matrix products  24.6 us (5%)
  between operations  14 us (3%)
  starting transfers between devices  8.87 us (2%)
    all_to_all x1, waiting for transfers between devices, shards(): lax.all_to_all(jnp.stack([jnp.concatenate([gate_weight, up_weight, down_w...  122 us
    reduce_scatter x1, waiting for transfers between devices, shards(): lax.psum_scatter(jnp.stack([partial_out, partial_in]).astype(jnp.bfloat16...  87.7 us
    scatter-add x3, other arithmetic, spread(): zero_block.at[:, block_lists.reshape(-1)]  57.1 us
    another operation x5, local copies, waits for them, and re-layouts  25.6 us
    reshape x3, local copies, waits for them, and re-layouts, spread(): contrib.reshape(rows_here, -1, BS)  25.1 us
    another operation x2, other arithmetic  15.6 us
  transfers between devices with their start and end apart: 4, of which 2 were waited for; matrix products, arithmetic and copies ran while one was open for 35% of the time, Pallas kernels for 0%

profile of v1, /device:TPU:2, one launch (start us, length us, event | category | flops | bytes accessed | tf_op | source)
XLA Modules:
  0.0 454.4 jit_solution(12689034781573418431)
XLA Ops:
  7.2 0.0 all-gather.2.cloned.1.call-start
  7.2 1.1 copy.75
  8.3 1.1 copy.76
  9.4 0.8 pad_maximum_fusion.2
  10.2 0.0 all-gather.2.cloned.1.call-update
  10.2 1.1 pad_maximum_fusion.3
  11.3 3.8 stack.11
  15.1 8.7 %all-to-all-start = ((bf16[16,21,64,128]{3,2,1,0:T(8,128)(2,1)}), bf16[16,21,64,128]{3,2,1,0:T(8,128)(2,1)}, u32[]{:S(2)}, u32[]{:S(2)}) async-start(bf16[16,21,64,128]{3,2,1,0:T(8,128)(2,1)} %stack.11), calls=%async_computation | async-start | bytes 11010048 | tf_op jit(solution)/shard_map/all_to_all | solution.py:26
  23.8 0.0 reduce-scatter.5.cloned.1.call-start
  23.9 0.1 reshape.196
  24.0 0.1 reshape.200
  24.1 0.1 reshape.193
  24.3 122.0 %all-to-all-done = bf16[16,21,64,128]{3,2,1,0:T(8,128)(2,1)} async-done(((bf16[16,21,64,128]{3,2,1,0:T(8,128)(2,1)}), bf16[16,21,64,128]{3,2,1,0:T(8,128)(2,1)}, u32[]{:S(2)}, u32[]{:S(2)}) %all-to-all-start) | async-done | bytes 5505056 | tf_op jit(solution)/shard_map/all_to_all | solution.py:26
  146.3 3.9 copy.127
  150.2 3.1 fusion.10
  153.3 5.7 %fusion.9 = (bf16[1,256,8192]{1,2,0:T(8,128)(2,1)}, bf16[1,256,8192]{1,2,0:T(8,128)(2,1)}) fusion(bf16[2,256,8192]{1,2,0:T(8,128)(2,1)} %all-gather.2.cloned.1.call-done), kind=kLoop, calls=%fused_computation.48 | loop fusion | bytes 16777216 | tf_op jit(solution)/shard_map/slice | solution.py:22
  159.0 6.4 %copy.77 = bf16[256,64,128]{2,0,1:T(8,128)(2,1)} copy(bf16[256,64,128]{0,2,1:T(8,128)(2,1)} %bitcast.110) | data formatting | bytes 8388608 | tf_op jit(solution)/shard_map/reshape;squeeze | solution.py:42
  165.4 6.4 %copy.84 = bf16[256,64,128]{2,0,1:T(8,128)(2,1)} copy(bf16[256,64,128]{0,2,1:T(8,128)(2,1)} %bitcast.109) | data formatting | bytes 8388608 | tf_op jit(solution)/shard_map/reshape;squeeze | solution.py:59
  171.7 5.1 %gather_fusion.1 = bf16[56,256,128]{2,1,0:T(8,128)(2,1)} fusion(bf16[256,64,128]{2,0,1:T(8,128)(2,1)} %copy.77, s32[1024]{0:T(1024)S(1)} %pad_clamp_fusion.1), kind=kCustom, calls=%fused_computation.1.clone | custom fusion | bytes 7340256 | tf_op jit(solution)/shard_map/jit(_take)/gather | solution.py:46
  176.8 5.1 %gather_fusion = bf16[56,256,128]{2,1,0:T(8,128)(2,1)} fusion(bf16[256,64,128]{2,0,1:T(8,128)(2,1)} %copy.77, s32[1024]{0:T(1024)S(1)} %pad_clamp_fusion.2), kind=kCustom, calls=%fused_computation.clone | custom fusion | bytes 7340256 | tf_op jit(solution)/shard_map/jit(_take)/gather | solution.py:43
  181.9 2.6 broadcast_select_fusion.1
  184.5 1.8 copy-done
  186.3 2.3 convolution_bitcast_fusion.1
  188.6 5.1 %gather_fusion.2 = bf16[56,256,128]{2,1,0:T(8,128)(2,1)} fusion(bf16[256,64,128]{2,0,1:T(8,128)(2,1)} %copy.84, s32[1024]{0:T(1024)S(1)} %pad_clamp_fusion), kind=kCustom, calls=%fused_computation.2.clone | custom fusion | bytes 7340256 | tf_op jit(solution)/shard_map/jit(_take)/gather | solution.py:60
  193.7 2.4 broadcast_select_fusion
  196.1 1.4 convolution_bitcast_fusion
  197.5 0.7 copy-done.3
  198.1 0.4 broadcast_select_fusion.2
  198.6 1.1 copy-done.4
  199.6 0.2 copy-done.5
  199.9 1.6 fusion.1
  201.5 1.4 convolution_convert_fusion.2
  202.8 0.7 copy-done.1
  203.5 1.4 convolution_convert_fusion.1
  204.9 1.4 convolution_convert_fusion
  206.2 2.9 pad_maximum_fusion.1
  209.1 0.0 reduce-scatter.5.cloned.1.call-update
  209.2 0.0 reduce-scatter.3.cloned.1.call-start
  209.2 0.1 reshape.203
  209.3 0.1 reshape.199
  209.4 0.1 reshape.189
  209.5 5.6 %fusion.13 = f32[7,8,128,256]{3,2,1,0:T(8,128)} fusion(bf16[7,8,128,128]{3,2,1,0:T(8,128)(2,1)} %bitcast.114, bf16[256,7,128,1]{0,2,3,1:T(8,128)(2,1)S(1)} %get-tuple-element.28), kind=kOutput, calls=%fused_computation.52 | convolution fusion | flops 469762048 | bytes 9633792 | tf_op jit(solution)/shard_map/tfi,fkri->tfkr/dot_general | solution.py:73
  215.1 8.4 %copy.89 = f32[256,56,128]{2,0,1:T(8,128)} copy(f32[256,56,128]{0,2,1:T(8,128)} %bitcast.101) | data formatting | bytes 14680064 | tf_op jit(solution)/shard_map/reshape | solution.py:16
  223.5 5.6 %fusion.4 = f32[7,8,128,256]{3,2,1,0:T(8,128)} fusion(bf16[7,8,128,128]{3,2,1,0:T(8,128)(2,1)} %bitcast.118, bf16[256,7,128]{0,2,1:T(8,128)(2,1)S(1)} %get-tuple-element.27), kind=kOutput, calls=%fused_computation.28 | convolution fusion | flops 469762048 | bytes 9633792 | tf_op jit(solution)/shard_map/tfi,fkri->tfkr/dot_general | solution.py:70
  229.1 8.4 %copy.87 = f32[256,56,128]{2,0,1:T(8,128)} copy(f32[256,56,128]{0,2,1:T(8,128)} %bitcast.102) | data formatting | bytes 14680064 | tf_op jit(solution)/shard_map/reshape | solution.py:16
  237.5 4.3 broadcast.59.clone.1
  241.7 19.1 %scatter_fusion.2 = f32[256,64,128]{2,0,1:T(8,128)} fusion(f32[256,64,128]{2,0,1:T(8,128)} %broadcast.59.clone.1, s32[56]{0:T(128)S(1)} %fusion.8, f32[56,256,128]{2,1,0:T(8,128)} %bitcast.104), kind=kCustom, calls=%fused_computation.5 | custom fusion | flops 1835008 | bytes 22020320 | tf_op jit(solution)/shard_map/scatter-add | solution.py:16
  260.8 4.3 broadcast.59.clone
  265.1 19.1 %scatter_fusion.1 = f32[256,64,128]{2,0,1:T(8,128)} fusion(f32[256,64,128]{2,0,1:T(8,128)} %broadcast.59.clone, s32[56]{0:T(128)S(1)} %fusion.7, f32[56,256,128]{2,1,0:T(8,128)} %bitcast.105), kind=kCustom, calls=%fused_computation.4 | custom fusion | flops 1835008 | bytes 22020320 | tf_op jit(solution)/shard_map/scatter-add | solution.py:16
  284.2 9.5 %add_convert_fusion = bf16[256,64,128]{2,0,1:T(8,128)(2,1)} fusion(f32[256,64,128]{2,0,1:T(8,128)} %scatter_fusion.1, f32[256,64,128]{2,0,1:T(8,128)} %scatter_fusion.2), kind=kLoop, calls=%fused_computation.7 | loop fusion | flops 4194304 | bytes 20971520 | tf_op jit(solution)/shard_map/convert.8
  293.7 6.4 %copy.90 = bf16[256,64,128]{0,2,1:T(8,128)(2,1)} copy(bf16[256,64,128]{2,0,1:T(8,128)(2,1)} %add_convert_fusion) | data formatting | bytes 8388608 | tf_op jit(solution)/shard_map/convert.8
  300.1 4.0 fusion.12
  304.2 8.3 %copy.82 = f32[256,56,128]{2,0,1:T(8,128)} copy(f32[256,56,128]{0,2,1:T(8,128)} %bitcast.103) | data formatting | bytes 14680064 | tf_op jit(solution)/shard_map/reshape | solution.py:16
  312.5 4.3 broadcast.59.clone.2
  316.8 18.9 %scatter_fusion = f32[256,64,128]{2,0,1:T(8,128)} fusion(f32[256,64,128]{2,0,1:T(8,128)} %broadcast.59.clone.2, s32[56]{0:T(128)S(1)} %fusion.6, f32[56,256,128]{2,1,0:T(8,128)} %bitcast.106), kind=kCustom, calls=%fused_computation.3 | custom fusion | flops 1835008 | bytes 22020320 | tf_op jit(solution)/shard_map/scatter-add | solution.py:16
  335.7 6.1 %convert.20 = bf16[256,64,128]{2,0,1:T(8,128)(2,1)} convert(f32[256,64,128]{2,0,1:T(8,128)} %scatter_fusion) | non-fusion elementwise | flops 2097152 | bytes 12582912 | tf_op jit(solution)/shard_map/convert.9
  341.8 6.4 %copy.83 = bf16[256,64,128]{0,2,1:T(8,128)(2,1)} copy(bf16[256,64,128]{2,0,1:T(8,128)(2,1)} %convert.20) | data formatting | bytes 8388608 | tf_op jit(solution)/shard_map/convert.9
  348.1 7.5 %pad_maximum_fusion = bf16[2,256,8192]{1,2,0:T(8,128)(2,1)} fusion(bf16[1,256,8192]{1,2,0:T(8,128)(2,1)} %bitcast.108, bf16[1,256,8192]{1,2,0:T(8,128)(2,1)} %bitcast.111), kind=kLoop, calls=%fused_computation.6 | loop fusion | flops 4194304 | bytes 16777216 | tf_op jit(solution)/shard_map/stack | solution.py:91
  355.6 0.0 reduce-scatter.5.cloned.1.call-done
  355.7 1.7 fusion.11
  357.4 87.7 %reduce-scatter.3.cloned.1.call-done = bf16[2,256,512]{1,2,0:T(8,128)(2,1)} async-done(((bf16[2,256,8192]{1,2,0:T(8,128)(2,1)}), bf16[2,256,512]{1,2,0:T(8,128)(2,1)}) %reduce-scatter.3.cloned.1.call-update) | async-done | bytes 524304 | tf_op jit(solution)/shard_map/reduce_scatter | solution.py:90
  445.1 1.1 slice_bitcast_fusion
  446.2 0.8 copy.97
  447.0 0.8 copy.98
  (27 shorter events, 0.1 us)
Async XLA Ops:
  7.2 146.1 %all-gather.2.cloned.1.call-start = ((), (), s32[]{:S(2)}) async-start(), calls=%async_computation.3 | async-start | bytes 8912896 | tf_op jit(solution)/shard_map/all_gather | solution.py:21
  15.1 8.8 %copy-start.6 = (s32[7,8]{1,0:T(8,128)S(1)}, s32[7,8]{1,0:T(8,128)}, u32[]{:S(2)}) copy-start(s32[7,8]{1,0:T(8,128)} %param.16) | copy-start | bytes 676
  15.1 8.9 %copy-start.8 = (s32[7,8]{1,0:T(8,128)S(1)}, s32[7,8]{1,0:T(8,128)}, u32[]{:S(2)}) copy-start(s32[7,8]{1,0:T(8,128)} %param.17) | copy-start | bytes 676
  15.1 9.0 %copy-start.7 = (s32[7,8]{1,0:T(8,128)S(1)}, s32[7,8]{1,0:T(8,128)}, u32[]{:S(2)}) copy-start(s32[7,8]{1,0:T(8,128)} %param.15) | copy-start | bytes 676
  15.1 131.2 %all-to-all-start = ((bf16[16,21,64,128]{3,2,1,0:T(8,128)(2,1)}), bf16[16,21,64,128]{3,2,1,0:T(8,128)(2,1)}, u32[]{:S(2)}, u32[]{:S(2)}) async-start(bf16[16,21,64,128]{3,2,1,0:T(8,128)(2,1)} %stack.11), calls=%async_computation | async-start | bytes 11010048 | tf_op jit(solution)/shard_map/all_to_all | solution.py:26
  23.8 331.8 %reduce-scatter.5.cloned.1.call-start = ((), (), s32[]{:S(2)}) async-start(), calls=%async_computation.5 | async-start | bytes 5849088 | tf_op jit(solution)/shard_map/reduce_scatter | solution.py:84
  181.9 4.4 copy-start.2
  184.5 1.8 copy-start
  196.1 2.0 copy-start.3
  198.1 1.5 copy-start.4
  198.1 1.7 copy-start.5
  201.5 2.0 copy-start.1
  209.2 235.9 %reduce-scatter.3.cloned.1.call-start = ((), (), s32[]{:S(2)}) async-start(), calls=%async_computation.4 | async-start | bytes 8912896 | tf_op jit(solution)/shard_map/reduce_scatter | solution.py:90
Sparse Core Ops, SparseCore 0:
  10.5 78.7 all-gather.1
  209.3 64.2 reduce-scatter.4
  355.7 89.2 reduce-scatter.2
